TPU v7x, 256 devices: a whole 4x4x8 slice. The times are simulated.
256 devices in a mesh: sub: 32 (over x, z_hi, core), coarse: 8 (over z_lo, y).
Axes of the slice: x: 4, y: 4, z: 8 (z_hi: 4, z_lo: 2; z = z_hi * 2 + z_lo), core: 2. Of those that a mesh axis runs over, the one named last changes fastest.
Arguments:
- residual_parts: bfloat16 [32, 8, 4, 256, 512], P('sub', 'coarse'), may hold values from -6 to 6
- face_slot: int32 [32, 8, 4], P('sub', 'coarse'), may hold values from 0 to 3, each once within a row
- face_order: int32 [32, 8, 4, 512], P('sub', 'coarse'), may hold values from 0 to 511, each once within a row
- face_scale: float32 [32, 8, 4], P('sub', 'coarse'), may hold values from 0 to 1, as said below
- vertex_unknowns: int32 [32, 8, 256], P('sub', 'coarse'), may hold values from 0 to 2047, all different within a row
- front_inverse: bfloat16 [32, 8, 2048, 2048], P('sub', 'coarse')
- coarse_basis: bfloat16 [32, 8, 2048, 256], P('sub', 'coarse'), may hold values from -0.125 to 0.125
- coarse_inverse: bfloat16 [32, 2048, 2048], P('sub', None, 'coarse'), as said below
- thermal_handoff: bfloat16 [32, 2048, 128], P('sub'), may hold values from -0.125 to 0.125
- chain_transfer: float32 [32, 128, 128], P('sub')
- coupling_in: bfloat16 [32, 128, 2048], P('sub', None, 'coarse'), may hold values from -0.5 to 0.5
Outputs:
- correction: bfloat16 [32, 8, 4, 256, 512], P('sub', 'coarse')
Inputs may be any that keep to these rules, and one draw needn't show every extreme that they name: `face_slot`: each row is a permutation of 0 to 3. `face_order`: each row is a permutation of 0 to 511. `vertex_unknowns`: the 256 entries of each subdomain are distinct. `face_scale`: the two weights of a shared face sum to one; a face on the outer boundary has weight one. `coarse_inverse`: each line's matrix is symmetric.
All inputs are finite; a program needn't handle non-finite values.
Results may differ from a plain program's by a relative error of at most 0.0059.
Values may be sent and summed in bfloat16 or wider, within the bound.
No kernel may reach another device: no remote copies, remote signals or barrier semaphores. Data moves between devices by JAX's collectives and lax.ppermute only.
A program may use at most 128 MiB of HBM per device.

v0:
```python
import jax
import jax.numpy as jnp
from jax import lax
from jax.sharding import PartitionSpec as P

HIGHEST = lax.Precision.HIGHEST


def with_halo(block, sides, width):
    for axis, dim in sides:
        count = lax.axis_size(axis)
        forward = [(i, i + 1) for i in range(count - 1)]
        backward = [(target, source) for source, target in forward]
        low = lax.ppermute(
            lax.slice_in_dim(block, block.shape[dim] - width, None, axis=dim), axis, forward
        )
        high = lax.ppermute(lax.slice_in_dim(block, 0, width, axis=dim), axis, backward)
        block = jnp.concatenate([low, block, high], axis=dim)
    return block


def carried_in(array, axis, combine, identity):
    peers, mine = (lax.axis_size(axis), lax.axis_index(axis))
    everything = jax.tree.map(lambda part: lax.all_gather(part, axis), array)
    start = jax.tree.map(
        lambda part, zero: jnp.broadcast_to(jnp.asarray(zero, part.dtype), part.shape),
        array,
        identity,
    )

    def step(k, before):
        reached = k < mine
        new = combine(before, jax.tree.map(lambda part: part[k], everything))
        return jax.tree.map(lambda a, b: jnp.where(reached, a, b), new, before)

    return lax.fori_loop(0, peers, step, start)


def build_tables(face_slot, face_order, table_type):
    face_count, block_size = face_order.shape
    slot_table = (
        face_slot[:, None] == lax.broadcasted_iota(jnp.int32, (face_count, face_count), 1)
    ).astype(table_type)
    order_table = (
        face_order[:, :, None]
        == lax.broadcasted_iota(jnp.int32, (face_count, block_size, block_size), 2)
    ).astype(table_type)
    return (slot_table, order_table)


def to_canonical(values, tables):
    slot_table, order_table = tables
    ordered = jnp.einsum(
        "snk,sjk->snj", values, order_table, preferred_element_type=jnp.float32, precision=HIGHEST
    ).astype(values.dtype)
    return jnp.einsum(
        "ds,snj->dnj", slot_table, ordered, preferred_element_type=jnp.float32, precision=HIGHEST
    ).astype(values.dtype)


def from_canonical(values, tables):
    slot_table, order_table = tables
    by_face = jnp.einsum(
        "ds,dnj->snj", slot_table, values, preferred_element_type=jnp.float32, precision=HIGHEST
    ).astype(values.dtype)
    return jnp.einsum(
        "snj,sjk->snk", by_face, order_table, preferred_element_type=jnp.float32, precision=HIGHEST
    ).astype(values.dtype)


def trade_faces(face_values):
    along_sub = with_halo(face_values[0:2], (("sub", 0),), 1)
    along_coarse = with_halo(face_values[2:4], (("coarse", 0),), 1)
    return jnp.stack([along_sub[0], along_sub[3], along_coarse[0], along_coarse[3]], 0)


def per_device(
    residual_parts,
    face_slot,
    face_order,
    face_scale,
    vertex_unknowns,
    front_inverse,
    coarse_basis,
    coarse_inverse,
    thermal_handoff,
    chain_transfer,
    coupling_in,
):
    own_parts = residual_parts[0, 0]
    own_slot = face_slot[0, 0]
    own_order = face_order[0, 0]
    own_scale = face_scale[0, 0][:, None, None]
    face_count, sample_count, block_size = own_parts.shape
    reduced_precision_tables = build_tables(own_slot, own_order, jnp.bfloat16)
    canon = to_canonical(own_parts, reduced_precision_tables)
    beside = trade_faces(canon)
    averaged = (own_scale * (canon.astype(jnp.float32) + beside.astype(jnp.float32))).astype(
        jnp.bfloat16
    )
    local_residual = from_canonical(averaged, reduced_precision_tables)
    own_primal = vertex_unknowns[0, 0]
    positions = lax.broadcasted_iota(jnp.int32, (own_primal.shape[0], face_count * block_size), 1)
    hits = jnp.sum((own_primal[:, None] == positions).astype(jnp.int32), axis=0)
    dual_mask = (1 - hits).astype(jnp.bfloat16).reshape(face_count, 1, block_size)
    inverse_blocks = front_inverse[0, 0].reshape(face_count, block_size, face_count, block_size)
    dual_part = (
        jnp.einsum(
            "gnj,gjfk->fnk",
            local_residual * dual_mask,
            inverse_blocks,
            preferred_element_type=jnp.float32,
        )
        * dual_mask
    )
    basis_blocks = coarse_basis[0, 0].reshape(face_count, block_size, -1)
    coarse_residual = jnp.einsum(
        "gnj,gjc->nc", local_residual, basis_blocks, preferred_element_type=jnp.float32
    ).astype(jnp.bfloat16)
    primal_count = coarse_residual.shape[1]
    line_block = coarse_inverse[0]
    line_outflow = thermal_handoff[0]
    channel_count = line_outflow.shape[1]
    line_base = lax.dot_general(
        line_block,
        lax.all_gather(coarse_residual, "coarse", axis=1, tiled=True),
        (((0,), (1,)), ((), ())),
        preferred_element_type=jnp.float32,
    )
    own_rows = lax.dynamic_slice_in_dim(
        line_outflow, lax.axis_index("coarse") * primal_count, primal_count, 0
    )
    inflow = lax.psum(
        jnp.dot(coarse_residual, own_rows, preferred_element_type=jnp.float32), "coarse"
    )
    transfer = chain_transfer[0]

    def compose(earlier, later):
        joined_map = jnp.dot(earlier[0], later[0], precision=HIGHEST)
        joined_state = jnp.dot(earlier[1], later[0], precision=HIGHEST) + later[1]
        return (joined_map, joined_state)

    identity = (jnp.eye(channel_count, dtype=jnp.float32), jnp.zeros_like(inflow))
    upstream_map, carried = carried_in((transfer, inflow), "sub", compose, identity)
    carried_term = lax.dot_general(
        coupling_in[0].astype(jnp.float32), carried, (((0,), (1,)), ((), ())), precision=HIGHEST
    )
    global_coarse_answer = (line_base + carried_term).astype(jnp.bfloat16)
    subregion_iterate = dual_part + jnp.einsum(
        "cn,gjc->gnj", global_coarse_answer, basis_blocks, preferred_element_type=jnp.float32
    )
    exact_tables = build_tables(own_slot, own_order, jnp.float32)
    weighted = (own_scale * to_canonical(subregion_iterate, exact_tables)).astype(jnp.bfloat16)
    beside_again = trade_faces(weighted)
    summed = (weighted.astype(jnp.float32) + beside_again.astype(jnp.float32)).astype(jnp.bfloat16)
    return from_canonical(summed, reduced_precision_tables)[None, None]


def solution(mesh):
    placed = (
        P("sub", "coarse", None, None, None),
        P("sub", "coarse", None),
        P("sub", "coarse", None, None),
        P("sub", "coarse", None),
        P("sub", "coarse", None),
        P("sub", "coarse", None, None),
        P("sub", "coarse", None, None),
        P("sub", None, "coarse"),
        P("sub", None, None),
        P("sub", None, None),
        P("sub", None, "coarse"),
    )
    return jax.shard_map(
        per_device,
        mesh=mesh,
        in_specs=placed,
        out_specs=P("sub", "coarse", None, None, None),
        check_vma=False,
    )
```

profile of v0, /device:TPU:26, one launch (start us, length us, event | category | flops | bytes accessed | tf_op | source)
XLA Modules:
  0.0 419.8 jit_solution(5209459540740825076)
XLA Ops:
  6.5 2.4 fusion.30
  11.1 2.3 fusion.70
  13.4 1.9 collective-permute-start
  15.4 7.6 %collective-permute-start.1 = (bf16[1,256,512]{2,0,1:T(2,128)(2,1)}, bf16[1,256,512]{2,0,1:T(2,128)(2,1)}, u32[]{:S(2)}, u32[]{:S(2)}) collective-permute-start(bf16[1,256,512]{2,0,1:T(2,128)(2,1)} %get-tuple-element.150), channel_id=1, source_target_pairs={{8,0},{16,8},{24,16},{32,24},{40,32},{48,40},{56,48},{64,56},{72,6... | collective-permute-start | bytes 786440 | tf_op jit(solution)/shard_map/ppermute | solution.py:17
  23.0 2.6 collective-permute-start.2
  25.6 3.3 collective-permute-start.3
  28.8 5.6 %collective-permute-done = bf16[1,256,512]{2,0,1:T(2,128)(2,1)} collective-permute-done((bf16[1,256,512]{2,0,1:T(2,128)(2,1)}, bf16[1,256,512]{2,0,1:T(2,128)(2,1)}, u32[]{:S(2)}, u32[]{:S(2)}) %collective-permute-start) | collective-permute-done | bytes 262176 | tf_op jit(solution)/shard_map/ppermute | solution.py:14
  34.5 1.2 collective-permute-done.1
  35.6 6.2 %collective-permute-done.2 = bf16[1,256,512]{2,0,1:T(2,128)(2,1)} collective-permute-done((bf16[1,256,512]{2,0,1:T(2,128)(2,1)S(1)}, bf16[1,256,512]{2,0,1:T(2,128)(2,1)}, u32[]{:S(2)}, u32[]{:S(2)}) %collective-permute-start.2) | collective-permute-done | bytes 262176 | tf_op jit(solution)/shard_map/ppermute | solution.py:14
  41.8 5.4 %collective-permute-done.3 = bf16[1,256,512]{2,0,1:T(2,128)(2,1)} collective-permute-done((bf16[1,256,512]{2,0,1:T(2,128)(2,1)S(1)}, bf16[1,256,512]{2,0,1:T(2,128)(2,1)}, u32[]{:S(2)}, u32[]{:S(2)}) %collective-permute-start.3) | collective-permute-done | bytes 262176 | tf_op jit(solution)/shard_map/ppermute | solution.py:17
  47.2 4.5 %convolution_convert_fusion.1 = bf16[4,256,512]{2,0,1:T(4,128)(2,1)S(1)} fusion(bf16[4,256,512]{2,0,1:T(4,128)(2,1)S(1)} %convolution_convert_fusion.2, bf16[1,256,512]{2,0,1:T(2,128)(2,1)} %collective-permute-done.3, bf16[1,256,512]{2,0,1:T(2,128)(2,1)} %collective-permute-done.2, bf16[1,256,512]{2,0,1:T(2,128)(2,1)} %collective-permute-done.1, ...), kind=kOutput, calls=%fused_computation.36 | convolution fusion | flops 11010064 | bytes 3145760 | tf_op jit(solution)/shard_map/ds,dnj->snj/dot_general | solution.py:63
  51.7 1.4 fusion.27
  54.5 1.7 convolution_bitcast_fusion.2
  57.9 75.5 %all-reduce.2.cloned.1.call-done = f32[1,256,128]{2,1,0:T(8,128)} async-done(((f32[1,256,128]{2,1,0:T(8,128)}), f32[1,256,128]{2,1,0:T(8,128)}) %all-reduce.2.cloned.1.call-update) | async-done | bytes 131088 | tf_op jit(solution)/shard_map/psum | solution.py:133
  133.9 14.5 %reshape_squeeze.6 = bf16[4,512,4,512]{3,2,1,0:T(4,128)(2,1)} reshape(bf16[1,1,2048,2048]{3,2,1,0:T(8,128)(2,1)} %param.18) | data formatting | bytes 16777216 | tf_op jit(solution)/shard_map/reshape;squeeze | solution.py:106
  148.4 6.5 %fusion.9 = f32[256,4,512,1]{2,0,3,1:T(8,128)S(1)} fusion(bf16[4,512,4,512]{3,2,1,0:T(4,128)(2,1)} %reshape_squeeze.6, bf16[4,256,512]{2,1,0:T(8,128)(2,1)} %copy-done.2, bf16[4,512]{1,0:T(4,128)(2,1)S(1)} %convert_element_type.89), kind=kOutput, calls=%fused_computation.11 | convolution fusion | flops 2149580800 | bytes 11538432 | tf_op jit(solution)/shard_map/gnj,gjfk->fnk/dot_general | solution.py:108
  155.0 22.1 %all-gather.4.cloned.1.call-done = bf16[256,2048]{1,0:T(8,128)(2,1)} async-done(((bf16[256,256]{1,0:T(8,128)(2,1)}), bf16[256,2048]{1,0:T(8,128)(2,1)}) %all-gather.4.cloned.1.call-update) | async-done | bytes 1048592 | tf_op jit(solution)/shard_map/all_gather | solution.py:126
  177.1 2.7 fusion.48
  179.8 54.5 %all-gather.6.cloned.1.call-done = f32[32,128,128]{2,1,0:T(8,128)} async-done(((f32[1,128,128]{2,1,0:T(8,128)}), f32[32,128,128]{2,1,0:T(8,128)}) %all-gather.6.cloned.1.call-update) | async-done | bytes 2097168 | tf_op jit(solution)/shard_map/all_gather | solution.py:24
  234.3 61.3 %all-gather.8.cloned.1.call-done = f32[32,256,128]{2,1,0:T(8,128)} async-done(((f32[1,256,128]{2,1,0:T(8,128)}), f32[32,256,128]{2,1,0:T(8,128)}) %all-gather.8.cloned.1.call-update) | async-done | bytes 4194320 | tf_op jit(solution)/shard_map/all_gather | solution.py:24
  295.6 71.3 %while.14 = (s32[]{:T(128)}, f32[256,128]{0,1:T(8,128)S(1)}, s32[]{:T(128)}, f32[32,128,128]{2,1,0:T(8,128)}, f32[32,256,128]{2,1,0:T(8,128)}, /*index=5*/s32[]{:T(128)}, s32[]{:T(128)}) while((s32[]{:T(128)}, f32[256,128]{0,1:T(8,128)S(1)}, s32[]{:T(128)}, f32[32,128,128]{2,1,0:T(8,128)}, f32[32,256,128]{2,1,0:T(8,128)}, ...), condition=%wide.region_3.4_spmd.clone, body=%wide.region_2.3_spmd.clone.sunk | while | flops 50462724 | bytes 1378403 | solution.py:36
  296.7 1.2 fusion.85
  298.9 1.2 fusion.85
  301.1 1.2 fusion.85
  303.3 1.2 fusion.85
  305.6 1.2 fusion.85
  307.8 1.2 fusion.85
  310.0 1.2 fusion.85
  312.2 1.2 fusion.85
  314.5 1.2 fusion.85
  316.7 1.2 fusion.85
  318.9 1.2 fusion.85
  321.2 1.2 fusion.85
  323.4 1.2 fusion.85
  325.6 1.2 fusion.85
  327.8 1.2 fusion.85
  330.1 1.2 fusion.85
  332.3 1.2 fusion.85
  334.5 1.2 fusion.85
  336.7 1.2 fusion.85
  339.0 1.2 fusion.85
  341.2 1.2 fusion.85
  343.4 1.2 fusion.85
  345.7 1.2 fusion.85
  347.9 1.2 fusion.85
  350.1 1.2 fusion.85
  352.3 1.2 fusion.85
  354.6 1.2 fusion.85
  356.8 1.2 fusion.85
  361.2 1.2 fusion.85
  365.7 1.2 fusion.85
  366.9 1.3 fusion.33
  368.7 2.8 fusion.12
  371.5 3.3 multiply_convert_fusion
  374.8 1.6 fusion.69
  376.4 2.2 collective-permute-start.4
  378.6 6.4 %collective-permute-start.5 = (bf16[1,256,512]{2,0,1:T(2,128)(2,1)S(1)}, bf16[1,256,512]{2,0,1:T(2,128)(2,1)S(1)}, u32[]{:S(2)}, u32[]{:S(2)}) collective-permute-start(bf16[1,256,512]{2,0,1:T(2,128)(2,1)S(1)} %get-tuple-element.146), channel_id=1, source_target_pairs={{8,0},{16,8},{24,16},{32,24},{40,32},{48,40},{56,48},{64,56},{72,6... | collective-permute-start | bytes 786440 | tf_op jit(solution)/shard_map/ppermute | solution.py:17
  385.0 2.1 collective-permute-start.6
  387.1 3.7 collective-permute-start.7
  390.9 5.8 %collective-permute-done.4 = bf16[1,256,512]{2,0,1:T(2,128)(2,1)S(1)} collective-permute-done((bf16[1,256,512]{2,0,1:T(2,128)(2,1)S(1)}, bf16[1,256,512]{2,0,1:T(2,128)(2,1)S(1)}, u32[]{:S(2)}, u32[]{:S(2)}) %collective-permute-start.4) | collective-permute-done | bytes 262176 | tf_op jit(solution)/shard_map/ppermute | solution.py:14
  397.1 5.4 %collective-permute-done.6 = bf16[1,256,512]{2,0,1:T(2,128)(2,1)S(1)} collective-permute-done((bf16[1,256,512]{2,0,1:T(2,128)(2,1)S(1)}, bf16[1,256,512]{2,0,1:T(2,128)(2,1)S(1)}, u32[]{:S(2)}, u32[]{:S(2)}) %collective-permute-start.6) | collective-permute-done | bytes 262176 | tf_op jit(solution)/shard_map/ppermute | solution.py:14
  402.4 5.8 %collective-permute-done.7 = bf16[1,256,512]{2,0,1:T(2,128)(2,1)S(1)} collective-permute-done((bf16[1,256,512]{2,0,1:T(2,128)(2,1)S(1)}, bf16[1,256,512]{2,0,1:T(2,128)(2,1)S(1)}, u32[]{:S(2)}, u32[]{:S(2)}) %collective-permute-start.7) | collective-permute-done | bytes 262176 | tf_op jit(solution)/shard_map/ppermute | solution.py:17
  408.2 2.9 convolution_convert_fusion
  411.1 2.2 fusion.29
  (134 shorter events, 41.5 us)
Async XLA Ops:
  6.5 46.5 %copy-start = (bf16[1,1,2048,256]{3,2,1,0:T(8,128)(2,1)S(1)}, bf16[1,1,2048,256]{3,2,1,0:T(8,128)(2,1)}, u32[]{:S(2)}) copy-start(bf16[1,1,2048,256]{3,2,1,0:T(8,128)(2,1)} %param.19) | copy-start | bytes 3145732
  6.5 126.9 %all-reduce.2.cloned.1.call-start = ((), (), s32[]{:S(2)}) async-start(), calls=%async_computation.2 | async-start | bytes 262144 | tf_op jit(solution)/shard_map/psum | solution.py:133
  6.5 3.5 copy-start.4
  11.1 36.1 %copy-start.7 = (f32[1,1,4]{2,1,0:T(1,128)S(1)}, f32[1,1,4]{2,1,0:T(1,128)}, u32[]{:S(2)}) copy-start(f32[1,1,4]{2,1,0:T(1,128)} %param.16) | copy-start | bytes 52
  13.4 21.0 %collective-permute-start = (bf16[1,256,512]{2,0,1:T(2,128)(2,1)}, bf16[1,256,512]{2,0,1:T(2,128)(2,1)}, u32[]{:S(2)}, u32[]{:S(2)}) collective-permute-start(bf16[1,256,512]{2,0,1:T(2,128)(2,1)} %get-tuple-element.147), channel_id=1, source_target_pairs={{0,8},{8,16},{16,24},{24,32},{32,40},{40,48},{48,56},{56,64},{64,7... | collective-permute-start | bytes 786440 | tf_op jit(solution)/shard_map/ppermute | solution.py:14
  15.4 20.3 %collective-permute-start.1 = (bf16[1,256,512]{2,0,1:T(2,128)(2,1)}, bf16[1,256,512]{2,0,1:T(2,128)(2,1)}, u32[]{:S(2)}, u32[]{:S(2)}) collective-permute-start(bf16[1,256,512]{2,0,1:T(2,128)(2,1)} %get-tuple-element.150), channel_id=1, source_target_pairs={{8,0},{16,8},{24,16},{32,24},{40,32},{48,40},{56,48},{64,56},{72,6... | collective-permute-start | bytes 786440 | tf_op jit(solution)/shard_map/ppermute | solution.py:17
  23.0 18.8 %collective-permute-start.2 = (bf16[1,256,512]{2,0,1:T(2,128)(2,1)S(1)}, bf16[1,256,512]{2,0,1:T(2,128)(2,1)}, u32[]{:S(2)}, u32[]{:S(2)}) collective-permute-start(bf16[1,256,512]{2,0,1:T(2,128)(2,1)S(1)} %get-tuple-element.149), channel_id=1, source_target_pairs={{0,1},{1,2},{2,3},{3,4},{4,5},{5,6},{6,7},{8,9},{9,10},{10,11},{11... | collective-permute-start | bytes 786440 | tf_op jit(solution)/shard_map/ppermute | solution.py:14
  25.6 21.6 %collective-permute-start.3 = (bf16[1,256,512]{2,0,1:T(2,128)(2,1)S(1)}, bf16[1,256,512]{2,0,1:T(2,128)(2,1)}, u32[]{:S(2)}, u32[]{:S(2)}) collective-permute-start(bf16[1,256,512]{2,0,1:T(2,128)(2,1)S(1)} %get-tuple-element.148), channel_id=1, source_target_pairs={{1,0},{2,1},{3,2},{4,3},{5,4},{6,5},{7,6},{9,8},{10,9},{11,10},{12... | collective-permute-start | bytes 786440 | tf_op jit(solution)/shard_map/ppermute | solution.py:17
  47.2 4.5 %copy-start.3 = (s32[1,1,4,512]{3,2,1,0:T(4,128)S(1)}, s32[1,1,4,512]{3,2,1,0:T(4,128)}, u32[]{:S(2)}) copy-start(s32[1,1,4,512]{3,2,1,0:T(4,128)} %param.15) | copy-start | bytes 24580
  53.1 1.0 copy-start.2
  53.1 80.5 %copy-start.6 = (s32[1,1,256]{2,1,0:T(1,128)S(1)}, s32[1,1,256]{2,1,0:T(1,128)}, u32[]{:S(2)}) copy-start(s32[1,1,256]{2,1,0:T(1,128)} %param.17) | copy-start | bytes 3076
  54.5 1.8 copy-start.1
  56.2 120.8 %all-gather.4.cloned.1.call-start = ((), (), s32[]{:S(2)}) async-start(), calls=%async_computation | async-start | bytes 1179648 | tf_op jit(solution)/shard_map/all_gather | solution.py:126
  57.0 177.3 %all-gather.6.cloned.1.call-start = ((), (), s32[]{:S(2)}) async-start(), calls=%async_computation.1 | async-start | bytes 2162688 | tf_op jit(solution)/shard_map/all_gather | solution.py:24
  57.7 237.9 %all-gather.8.cloned.1.call-start = ((), (), s32[]{:S(2)}) async-start(), calls=%async_computation.3 | async-start | bytes 4325376 | tf_op jit(solution)/shard_map/all_gather | solution.py:24
  368.7 2.8 copy-start.5
  368.7 2.8 copy-start.8
  376.4 20.3 %collective-permute-start.4 = (bf16[1,256,512]{2,0,1:T(2,128)(2,1)S(1)}, bf16[1,256,512]{2,0,1:T(2,128)(2,1)S(1)}, u32[]{:S(2)}, u32[]{:S(2)}) collective-permute-start(bf16[1,256,512]{2,0,1:T(2,128)(2,1)S(1)} %get-tuple-element.143), channel_id=1, source_target_pairs={{0,8},{8,16},{16,24},{24,32},{32,40},{40,48},{48,56},{56,64},{64,7... | collective-permute-start | bytes 786440 | tf_op jit(solution)/shard_map/ppermute | solution.py:14
  378.6 18.5 %collective-permute-start.5 = (bf16[1,256,512]{2,0,1:T(2,128)(2,1)S(1)}, bf16[1,256,512]{2,0,1:T(2,128)(2,1)S(1)}, u32[]{:S(2)}, u32[]{:S(2)}) collective-permute-start(bf16[1,256,512]{2,0,1:T(2,128)(2,1)S(1)} %get-tuple-element.146), channel_id=1, source_target_pairs={{8,0},{16,8},{24,16},{32,24},{40,32},{48,40},{56,48},{64,56},{72,6... | collective-permute-start | bytes 786440 | tf_op jit(solution)/shard_map/ppermute | solution.py:17
  385.0 17.5 %collective-permute-start.6 = (bf16[1,256,512]{2,0,1:T(2,128)(2,1)S(1)}, bf16[1,256,512]{2,0,1:T(2,128)(2,1)S(1)}, u32[]{:S(2)}, u32[]{:S(2)}) collective-permute-start(bf16[1,256,512]{2,0,1:T(2,128)(2,1)S(1)} %get-tuple-element.145), channel_id=1, source_target_pairs={{0,1},{1,2},{2,3},{3,4},{4,5},{5,6},{6,7},{8,9},{9,10},{10,11},{11... | collective-permute-start | bytes 786440 | tf_op jit(solution)/shard_map/ppermute | solution.py:14
  387.1 21.1 %collective-permute-start.7 = (bf16[1,256,512]{2,0,1:T(2,128)(2,1)S(1)}, bf16[1,256,512]{2,0,1:T(2,128)(2,1)S(1)}, u32[]{:S(2)}, u32[]{:S(2)}) collective-permute-start(bf16[1,256,512]{2,0,1:T(2,128)(2,1)S(1)} %get-tuple-element.144), channel_id=1, source_target_pairs={{1,0},{2,1},{3,2},{4,3},{5,4},{6,5},{7,6},{9,8},{10,9},{11,10},{12... | collective-permute-start | bytes 786440 | tf_op jit(solution)/shard_map/ppermute | solution.py:17
Sparse Core Ops, SparseCore 0:
  56.3 77.0 all-reduce.1
  135.3 41.7 all-gather.3
  180.0 54.2 all-gather.5
  237.0 58.5 all-gather.7
where the time goes:
time: 423 us; the launch traced here: 420 us
  waiting for transfers between devices  251 us (59%)
  matrix products  70.6 us (17%)
  local copies, waits for them, and re-layouts  53.2 us (13%)
  starting transfers between devices  30.1 us (7%)
  between operations  13.4 us (3%)
    all_gather x2, waiting for transfers between devices, carried_in(): everything = jax.tree.map(lambda part: lax.all_gather(part, axis), array)  116 us
    psum x1, waiting for transfers between devices, per_device(): lax.psum(jnp.dot(coarse_residual, own_rows, preferred_element_type=jnp.fl...  75.5 us
    dot_general x32, matrix products, compose(): joined_state = jnp.dot(earlier[1], later[0], precision=HIGHEST) + later[1]  37 us
    dynamic_slice x64, local copies, waits for them, and re-layouts, step(): new = combine(before, jax.tree.map(lambda part: part[k], everything))  32.4 us
    ppermute x4, waiting for transfers between devices, with_halo(): lax.ppermute(lax.slice_in_dim(block, block.shape[dim] - width, None, axis...  23 us
    all_gather x1, waiting for transfers between devices, per_device(): lax.all_gather(coarse_residual, 'coarse', axis=1, tiled=True)  22.1 us
    ppermute x4, starting transfers between devices, with_halo(): lax.ppermute(lax.slice_in_dim(block, 0, width, axis=dim), axis, backward)  21 us
    another operation x1, local copies, waits for them, and re-layouts, per_device(): front_inverse[0, 0].reshape(face_count, block_size, face_count, block_size)  14.5 us
  transfers between devices with their start and end apart: 12, of which 12 were waited for; matrix products, arithmetic and copies ran while one was open for 6% of the time, Pallas kernels for 0%

commit v1 on v0

--- a/solution.py
+++ b/solution.py
@@ -123,7 +123,10 @@
     channel_count = line_outflow.shape[1]
     line_base = lax.dot_general(
         line_block,
-        lax.all_gather(coarse_residual, "coarse", axis=1, tiled=True),
+        jnp.concatenate(
+            lax.all_to_all(jnp.stack([coarse_residual] * lax.axis_size("coarse")), "coarse", 0, 0),
+            axis=1,
+        ),
         (((0,), (1,)), ((), ())),
         preferred_element_type=jnp.float32,
     )

time: 423 us -> 325 us (0.77)
  waiting for transfers between devices: 251 us -> 145 us
  starting transfers between devices: 30.1 us -> 36.1 us
    all_gather x2, waiting for transfers between devices: 116 us -> 31.2 us  [carried_in(): everything = jax.tree.map(lambda part: lax.all_gather(part, axis), array)]
    all_gather x1 -> x0, waiting for transfers between devices: 22.1 us -> none  [per_device(): lax.all_gather(coarse_residual, 'coarse', axis=1, tiled=True)]
    all_to_all x0 -> x1, starting transfers between devices: none -> 6.2 us  [per_device(): lax.all_to_all(jnp.stack([coarse_residual] * lax.axis_size('coarse')), 'c...]
  transfers between devices with their start and end apart: 12 -> 12, of which waited for: 12 -> 9; matrix products, arithmetic and copies ran while one was open for 6% -> 8% of each run, Pallas kernels for 0% -> 0%
where the time goes in v1:
time: 325 us; the launch traced here: 323 us
  waiting for transfers between devices  145 us (45%)
  matrix products  68.8 us (21%)
  local copies, waits for them, and re-layouts  55.2 us (17%)
  starting transfers between devices  36.1 us (11%)
  between operations  15.1 us (5%)
    psum x1, waiting for transfers between devices, per_device(): lax.psum(jnp.dot(coarse_residual, own_rows, preferred_element_type=jnp.fl...  76.7 us
    dot_general x32, matrix products, compose(): joined_state = jnp.dot(earlier[1], later[0], precision=HIGHEST) + later[1]  37 us
    dynamic_slice x64, local copies, waits for them, and re-layouts, step(): new = combine(before, jax.tree.map(lambda part: part[k], everything))  32.4 us
    all_gather x2, waiting for transfers between devices, carried_in(): everything = jax.tree.map(lambda part: lax.all_gather(part, axis), array)  31.2 us
    ppermute x4, waiting for transfers between devices, with_halo(): lax.ppermute(lax.slice_in_dim(block, block.shape[dim] - width, None, axis...  23.1 us
    ppermute x4, starting transfers between devices, with_halo(): lax.ppermute(lax.slice_in_dim(block, 0, width, axis=dim), axis, backward)  20.5 us
    another operation x1, local copies, waits for them, and re-layouts, per_device(): front_inverse[0, 0].reshape(face_count, block_size, face_count, block_size)  14.6 us
    ppermute x4, waiting for transfers between devices, with_halo(): lax.ppermute(lax.slice_in_dim(block, 0, width, axis=dim), axis, backward)  14 us
  transfers between devices with their start and end apart: 12, of which 9 were waited for; matrix products, arithmetic and copies ran while one was open for 8% of the time, Pallas kernels for 0%

profile of v1, /device:TPU:26, one launch (start us, length us, event | category | flops | bytes accessed | tf_op | source)
XLA Modules:
  0.0 322.6 jit_solution(11677442273700182877)
XLA Ops:
  7.4 2.4 fusion.30
  10.8 1.1 convolution_convert_fusion.2
  11.9 2.3 fusion.70
  14.3 1.9 collective-permute-start
  16.2 7.6 %collective-permute-start.1 = (bf16[1,256,512]{2,0,1:T(2,128)(2,1)}, bf16[1,256,512]{2,0,1:T(2,128)(2,1)}, u32[]{:S(2)}, u32[]{:S(2)}) collective-permute-start(bf16[1,256,512]{2,0,1:T(2,128)(2,1)} %get-tuple-element.155), channel_id=1, source_target_pairs={{8,0},{16,8},{24,16},{32,24},{40,32},{48,40},{56,48},{64,56},{72,6... | collective-permute-start | bytes 786440 | tf_op jit(solution)/shard_map/ppermute | solution.py:17
  23.8 2.6 collective-permute-start.2
  26.4 3.3 %collective-permute-start.3 = (bf16[1,256,512]{2,0,1:T(2,128)(2,1)S(1)}, bf16[1,256,512]{2,0,1:T(2,128)(2,1)}, u32[]{:S(2)}, u32[]{:S(2)}) collective-permute-start(bf16[1,256,512]{2,0,1:T(2,128)(2,1)S(1)} %get-tuple-element.153), channel_id=1, source_target_pairs={{1,0},{2,1},{3,2},{4,3},{5,4},{6,5},{7,6},{9,8},{10,9},{11,10},{12... | collective-permute-start | bytes 786440 | tf_op jit(solution)/shard_map/ppermute | solution.py:17
  29.7 5.6 %collective-permute-done = bf16[1,256,512]{2,0,1:T(2,128)(2,1)} collective-permute-done((bf16[1,256,512]{2,0,1:T(2,128)(2,1)}, bf16[1,256,512]{2,0,1:T(2,128)(2,1)}, u32[]{:S(2)}, u32[]{:S(2)}) %collective-permute-start) | collective-permute-done | bytes 262176 | tf_op jit(solution)/shard_map/ppermute | solution.py:14
  35.3 1.2 collective-permute-done.1
  36.5 6.2 %collective-permute-done.2 = bf16[1,256,512]{2,0,1:T(2,128)(2,1)} collective-permute-done((bf16[1,256,512]{2,0,1:T(2,128)(2,1)S(1)}, bf16[1,256,512]{2,0,1:T(2,128)(2,1)}, u32[]{:S(2)}, u32[]{:S(2)}) %collective-permute-start.2) | collective-permute-done | bytes 262176 | tf_op jit(solution)/shard_map/ppermute | solution.py:14
  42.7 5.4 %collective-permute-done.3 = bf16[1,256,512]{2,0,1:T(2,128)(2,1)} collective-permute-done((bf16[1,256,512]{2,0,1:T(2,128)(2,1)S(1)}, bf16[1,256,512]{2,0,1:T(2,128)(2,1)}, u32[]{:S(2)}, u32[]{:S(2)}) %collective-permute-start.3) | collective-permute-done | bytes 262176 | tf_op jit(solution)/shard_map/ppermute | solution.py:17
  48.0 4.5 %convolution_convert_fusion.1 = bf16[4,256,512]{2,0,1:T(4,128)(2,1)S(1)} fusion(bf16[4,256,512]{2,0,1:T(4,128)(2,1)S(1)} %convolution_convert_fusion.2, bf16[1,256,512]{2,0,1:T(2,128)(2,1)} %collective-permute-done.3, bf16[1,256,512]{2,0,1:T(2,128)(2,1)} %collective-permute-done.2, bf16[1,256,512]{2,0,1:T(2,128)(2,1)} %collective-permute-done.1, ...), kind=kOutput, calls=%fused_computation.36 | convolution fusion | flops 11010064 | bytes 3145760 | tf_op jit(solution)/shard_map/ds,dnj->snj/dot_general | solution.py:63
  52.5 1.4 fusion.27
  55.4 1.7 convolution_bitcast_fusion.2
  57.7 76.7 %all-reduce.2.cloned.1.call-done = f32[1,256,128]{2,1,0:T(8,128)} async-done(((f32[1,256,128]{2,1,0:T(8,128)}), f32[1,256,128]{2,1,0:T(8,128)}) %all-reduce.2.cloned.1.call-update) | async-done | bytes 131088 | tf_op jit(solution)/shard_map/psum | solution.py:136
  135.5 6.2 %all-to-all-start = ((bf16[8,256,256]{1,2,0:T(8,128)(2,1)}), bf16[8,256,256]{1,2,0:T(8,128)(2,1)S(1)}, u32[]{:S(2)}, u32[]{:S(2)}) async-start(bf16[8,256,256]{1,2,0:T(8,128)(2,1)} %stack.7), calls=%async_computation | async-start | bytes 2097152 | tf_op jit(solution)/shard_map/all_to_all | solution.py:127
  142.1 14.6 %reshape_squeeze.6 = bf16[4,512,4,512]{3,2,1,0:T(4,128)(2,1)} reshape(bf16[1,1,2048,2048]{3,2,1,0:T(8,128)(2,1)} %param.18) | data formatting | bytes 16777216 | tf_op jit(solution)/shard_map/reshape;squeeze | solution.py:106
  156.7 7.9 %fusion.9 = f32[256,4,512,1]{2,0,3,1:T(8,128)} fusion(bf16[4,512,4,512]{3,2,1,0:T(4,128)(2,1)} %reshape_squeeze.6, bf16[4,256,512]{2,1,0:T(8,128)(2,1)} %copy-done.3, bf16[4,512]{1,0:T(4,128)(2,1)S(1)} %convert_element_type.89), kind=kOutput, calls=%fused_computation.11 | convolution fusion | flops 2149580800 | bytes 11538432 | tf_op jit(solution)/shard_map/gnj,gjfk->fnk/dot_general | solution.py:108
  165.1 31.2 %all-gather.5.cloned.1.call-done = f32[32,256,128]{2,1,0:T(8,128)} async-done(((f32[1,256,128]{2,1,0:T(8,128)}), f32[32,256,128]{2,1,0:T(8,128)}) %all-gather.5.cloned.1.call-update) | async-done | bytes 4194320 | tf_op jit(solution)/shard_map/all_gather | solution.py:24
  196.3 71.3 %while.14 = (s32[]{:T(128)}, f32[256,128]{0,1:T(8,128)S(1)}, s32[]{:T(128)}, f32[32,128,128]{2,1,0:T(8,128)}, f32[32,256,128]{2,1,0:T(8,128)}, /*index=5*/s32[]{:T(128)}, s32[]{:T(128)}) while((s32[]{:T(128)}, f32[256,128]{0,1:T(8,128)S(1)}, s32[]{:T(128)}, f32[32,128,128]{2,1,0:T(8,128)}, f32[32,256,128]{2,1,0:T(8,128)}, ...), condition=%wide.region_3.4_spmd.clone, body=%wide.region_2.3_spmd.clone.sunk | while | flops 50462724 | bytes 1378403 | solution.py:36
  197.4 1.2 fusion.85
  199.6 1.2 fusion.85
  201.8 1.2 fusion.85
  204.1 1.2 fusion.85
  206.3 1.2 fusion.85
  208.5 1.2 fusion.85
  210.8 1.2 fusion.85
  213.0 1.2 fusion.85
  215.2 1.2 fusion.85
  217.4 1.2 fusion.85
  219.7 1.2 fusion.85
  221.9 1.2 fusion.85
  224.1 1.2 fusion.85
  226.3 1.2 fusion.85
  228.6 1.2 fusion.85
  230.8 1.2 fusion.85
  233.0 1.2 fusion.85
  235.3 1.2 fusion.85
  237.5 1.2 fusion.85
  239.7 1.2 fusion.85
  241.9 1.2 fusion.85
  244.2 1.2 fusion.85
  246.4 1.2 fusion.85
  248.6 1.2 fusion.85
  250.8 1.2 fusion.85
  253.1 1.2 fusion.85
  255.3 1.2 fusion.85
  257.5 1.2 fusion.85
  259.8 1.2 fusion.85
  262.0 1.2 fusion.85
  264.2 1.2 fusion.85
  266.4 1.2 fusion.85
  269.2 2.7 fusion.12
  272.0 3.3 %multiply_convert_fusion = bf16[4,256,512]{2,0,1:T(4,128)(2,1)S(1)} fusion(f32[4,256,512]{2,1,0:T(8,128)S(1)} %fusion.12, f32[4]{0:T(128)S(1)} %bitcast.94, s32[4]{0:T(128)S(1)} %bitcast.90), kind=kOutput, calls=%fused_computation.24 | convolution fusion | flops 26214416 | bytes 3145760 | tf_op jit(solution)/shard_map/ds,snj->dnj/dot_general | solution.py:56
  275.3 1.6 fusion.69
  276.9 2.2 collective-permute-start.4
  279.1 6.4 %collective-permute-start.5 = (bf16[1,256,512]{2,0,1:T(2,128)(2,1)S(1)}, bf16[1,256,512]{2,0,1:T(2,128)(2,1)S(1)}, u32[]{:S(2)}, u32[]{:S(2)}) collective-permute-start(bf16[1,256,512]{2,0,1:T(2,128)(2,1)S(1)} %get-tuple-element.151), channel_id=1, source_target_pairs={{8,0},{16,8},{24,16},{32,24},{40,32},{48,40},{56,48},{64,56},{72,6... | collective-permute-start | bytes 786440 | tf_op jit(solution)/shard_map/ppermute | solution.py:17
  285.5 2.6 collective-permute-start.6
  288.1 3.3 %collective-permute-start.7 = (bf16[1,256,512]{2,0,1:T(2,128)(2,1)S(1)}, bf16[1,256,512]{2,0,1:T(2,128)(2,1)S(1)}, u32[]{:S(2)}, u32[]{:S(2)}) collective-permute-start(bf16[1,256,512]{2,0,1:T(2,128)(2,1)S(1)} %get-tuple-element.149), channel_id=1, source_target_pairs={{1,0},{2,1},{3,2},{4,3},{5,4},{6,5},{7,6},{9,8},{10,9},{11,10},{12... | collective-permute-start | bytes 786440 | tf_op jit(solution)/shard_map/ppermute | solution.py:17
  291.3 6.7 %collective-permute-done.4 = bf16[1,256,512]{2,0,1:T(2,128)(2,1)S(1)} collective-permute-done((bf16[1,256,512]{2,0,1:T(2,128)(2,1)S(1)}, bf16[1,256,512]{2,0,1:T(2,128)(2,1)S(1)}, u32[]{:S(2)}, u32[]{:S(2)}) %collective-permute-start.4) | collective-permute-done | bytes 262176 | tf_op jit(solution)/shard_map/ppermute | solution.py:14
  298.1 4.6 %collective-permute-done.6 = bf16[1,256,512]{2,0,1:T(2,128)(2,1)S(1)} collective-permute-done((bf16[1,256,512]{2,0,1:T(2,128)(2,1)S(1)}, bf16[1,256,512]{2,0,1:T(2,128)(2,1)S(1)}, u32[]{:S(2)}, u32[]{:S(2)}) %collective-permute-start.6) | collective-permute-done | bytes 262176 | tf_op jit(solution)/shard_map/ppermute | solution.py:14
  302.6 7.4 %collective-permute-done.7 = bf16[1,256,512]{2,0,1:T(2,128)(2,1)S(1)} collective-permute-done((bf16[1,256,512]{2,0,1:T(2,128)(2,1)S(1)}, bf16[1,256,512]{2,0,1:T(2,128)(2,1)S(1)}, u32[]{:S(2)}, u32[]{:S(2)}) %collective-permute-start.7) | collective-permute-done | bytes 262176 | tf_op jit(solution)/shard_map/ppermute | solution.py:17
  310.0 2.9 convolution_convert_fusion
  313.0 2.2 fusion.29
  (139 shorter events, 39.4 us)
Async XLA Ops:
  7.4 46.5 %copy-start = (bf16[1,1,2048,256]{3,2,1,0:T(8,128)(2,1)S(1)}, bf16[1,1,2048,256]{3,2,1,0:T(8,128)(2,1)}, u32[]{:S(2)}) copy-start(bf16[1,1,2048,256]{3,2,1,0:T(8,128)(2,1)} %param.19) | copy-start | bytes 3145732
  7.4 127.0 %all-reduce.2.cloned.1.call-start = ((), (), s32[]{:S(2)}) async-start(), calls=%async_computation.2 | async-start | bytes 262144 | tf_op jit(solution)/shard_map/psum | solution.py:136
  7.4 3.5 %copy-start.6 = (s32[1,1,4]{2,1,0:T(1,128)S(1)}, s32[1,1,4]{2,1,0:T(1,128)}, u32[]{:S(2)}) copy-start(s32[1,1,4]{2,1,0:T(1,128)} %param.14) | copy-start | bytes 52
  11.9 36.1 %copy-start.9 = (f32[1,1,4]{2,1,0:T(1,128)S(1)}, f32[1,1,4]{2,1,0:T(1,128)}, u32[]{:S(2)}) copy-start(f32[1,1,4]{2,1,0:T(1,128)} %param.16) | copy-start | bytes 52
  14.3 21.0 %collective-permute-start = (bf16[1,256,512]{2,0,1:T(2,128)(2,1)}, bf16[1,256,512]{2,0,1:T(2,128)(2,1)}, u32[]{:S(2)}, u32[]{:S(2)}) collective-permute-start(bf16[1,256,512]{2,0,1:T(2,128)(2,1)} %get-tuple-element.152), channel_id=1, source_target_pairs={{0,8},{8,16},{16,24},{24,32},{32,40},{40,48},{48,56},{56,64},{64,7... | collective-permute-start | bytes 786440 | tf_op jit(solution)/shard_map/ppermute | solution.py:14
  16.2 20.3 %collective-permute-start.1 = (bf16[1,256,512]{2,0,1:T(2,128)(2,1)}, bf16[1,256,512]{2,0,1:T(2,128)(2,1)}, u32[]{:S(2)}, u32[]{:S(2)}) collective-permute-start(bf16[1,256,512]{2,0,1:T(2,128)(2,1)} %get-tuple-element.155), channel_id=1, source_target_pairs={{8,0},{16,8},{24,16},{32,24},{40,32},{48,40},{56,48},{64,56},{72,6... | collective-permute-start | bytes 786440 | tf_op jit(solution)/shard_map/ppermute | solution.py:17
  23.8 18.8 %collective-permute-start.2 = (bf16[1,256,512]{2,0,1:T(2,128)(2,1)S(1)}, bf16[1,256,512]{2,0,1:T(2,128)(2,1)}, u32[]{:S(2)}, u32[]{:S(2)}) collective-permute-start(bf16[1,256,512]{2,0,1:T(2,128)(2,1)S(1)} %get-tuple-element.154), channel_id=1, source_target_pairs={{0,1},{1,2},{2,3},{3,4},{4,5},{5,6},{6,7},{8,9},{9,10},{10,11},{11... | collective-permute-start | bytes 786440 | tf_op jit(solution)/shard_map/ppermute | solution.py:14
  26.4 21.6 %collective-permute-start.3 = (bf16[1,256,512]{2,0,1:T(2,128)(2,1)S(1)}, bf16[1,256,512]{2,0,1:T(2,128)(2,1)}, u32[]{:S(2)}, u32[]{:S(2)}) collective-permute-start(bf16[1,256,512]{2,0,1:T(2,128)(2,1)S(1)} %get-tuple-element.153), channel_id=1, source_target_pairs={{1,0},{2,1},{3,2},{4,3},{5,4},{6,5},{7,6},{9,8},{10,9},{11,10},{12... | collective-permute-start | bytes 786440 | tf_op jit(solution)/shard_map/ppermute | solution.py:17
  48.0 4.5 %copy-start.5 = (s32[1,1,4,512]{3,2,1,0:T(4,128)S(1)}, s32[1,1,4,512]{3,2,1,0:T(4,128)}, u32[]{:S(2)}) copy-start(s32[1,1,4,512]{3,2,1,0:T(4,128)} %param.15) | copy-start | bytes 24580
  53.9 1.0 copy-start.3
  55.3 86.4 %copy-start.8 = (s32[1,1,256]{2,1,0:T(1,128)S(1)}, s32[1,1,256]{2,1,0:T(1,128)}, u32[]{:S(2)}) copy-start(s32[1,1,256]{2,1,0:T(1,128)} %param.17) | copy-start | bytes 3076
  57.1 108.1 %all-gather.3.cloned.1.call-start = ((), (), s32[]{:S(2)}) async-start(), calls=%async_computation.1 | async-start | bytes 2162688 | tf_op jit(solution)/shard_map/all_gather | solution.py:24
  57.6 138.7 %all-gather.5.cloned.1.call-start = ((), (), s32[]{:S(2)}) async-start(), calls=%async_computation.3 | async-start | bytes 4325376 | tf_op jit(solution)/shard_map/all_gather | solution.py:24
  135.5 29.1 %all-to-all-start = ((bf16[8,256,256]{1,2,0:T(8,128)(2,1)}), bf16[8,256,256]{1,2,0:T(8,128)(2,1)S(1)}, u32[]{:S(2)}, u32[]{:S(2)}) async-start(bf16[8,256,256]{1,2,0:T(8,128)(2,1)} %stack.7), calls=%async_computation | async-start | bytes 2097152 | tf_op jit(solution)/shard_map/all_to_all | solution.py:127
  156.7 8.0 %copy-start.2 = (bf16[1,2048,256]{2,1,0:T(8,128)(2,1)S(1)}, bf16[1,2048,256]{2,1,0:T(8,128)(2,1)}, u32[]{:S(2)}) copy-start(bf16[1,2048,256]{2,1,0:T(8,128)(2,1)} %param.20) | copy-start | bytes 3145732
  196.3 71.3 %copy-start.4 = (bf16[1,128,256]{2,1,0:T(8,128)(2,1)S(1)}, bf16[1,128,256]{2,1,0:T(8,128)(2,1)}, u32[]{:S(2)}) copy-start(bf16[1,128,256]{2,1,0:T(8,128)(2,1)} %param.23) | copy-start | bytes 196612
  267.6 1.6 copy-start.1
  269.2 2.8 copy-start.7
  269.2 2.8 copy-start.10
  276.9 21.2 %collective-permute-start.4 = (bf16[1,256,512]{2,0,1:T(2,128)(2,1)S(1)}, bf16[1,256,512]{2,0,1:T(2,128)(2,1)S(1)}, u32[]{:S(2)}, u32[]{:S(2)}) collective-permute-start(bf16[1,256,512]{2,0,1:T(2,128)(2,1)S(1)} %get-tuple-element.148), channel_id=1, source_target_pairs={{0,8},{8,16},{16,24},{24,32},{32,40},{40,48},{48,56},{56,64},{64,7... | collective-permute-start | bytes 786440 | tf_op jit(solution)/shard_map/ppermute | solution.py:14
  279.1 19.0 %collective-permute-start.5 = (bf16[1,256,512]{2,0,1:T(2,128)(2,1)S(1)}, bf16[1,256,512]{2,0,1:T(2,128)(2,1)S(1)}, u32[]{:S(2)}, u32[]{:S(2)}) collective-permute-start(bf16[1,256,512]{2,0,1:T(2,128)(2,1)S(1)} %get-tuple-element.151), channel_id=1, source_target_pairs={{8,0},{16,8},{24,16},{32,24},{40,32},{48,40},{56,48},{64,56},{72,6... | collective-permute-start | bytes 786440 | tf_op jit(solution)/shard_map/ppermute | solution.py:17
  285.5 17.1 %collective-permute-start.6 = (bf16[1,256,512]{2,0,1:T(2,128)(2,1)S(1)}, bf16[1,256,512]{2,0,1:T(2,128)(2,1)S(1)}, u32[]{:S(2)}, u32[]{:S(2)}) collective-permute-start(bf16[1,256,512]{2,0,1:T(2,128)(2,1)S(1)} %get-tuple-element.150), channel_id=1, source_target_pairs={{0,1},{1,2},{2,3},{3,4},{4,5},{5,6},{6,7},{8,9},{9,10},{10,11},{11... | collective-permute-start | bytes 786440 | tf_op jit(solution)/shard_map/ppermute | solution.py:14
  288.1 22.0 %collective-permute-start.7 = (bf16[1,256,512]{2,0,1:T(2,128)(2,1)S(1)}, bf16[1,256,512]{2,0,1:T(2,128)(2,1)S(1)}, u32[]{:S(2)}, u32[]{:S(2)}) collective-permute-start(bf16[1,256,512]{2,0,1:T(2,128)(2,1)S(1)} %get-tuple-element.149), channel_id=1, source_target_pairs={{1,0},{2,1},{3,2},{4,3},{5,4},{6,5},{7,6},{9,8},{10,9},{11,10},{12... | collective-permute-start | bytes 786440 | tf_op jit(solution)/shard_map/ppermute | solution.py:17
Sparse Core Ops, SparseCore 0:
  57.2 77.1 all-reduce.1
Sparse Core Ops, SparseCore 1:
  60.1 54.1 all-gather.2
  134.5 61.8 all-gather.4
